TPU v7x, 256 devices: a whole 4x4x8 slice. The times are simulated.
256 devices in a mesh: tp: 8 (over x, z_lo), wide: 32 (over y, z_hi, core).
Axes of the slice: x: 4, y: 4, z: 8 (z_hi: 4, z_lo: 2; z = z_hi * 2 + z_lo), core: 2. Of those that a mesh axis runs over, the one named last changes fastest.
Arguments:
- token_keys: bfloat16 [4096, 28672], P('tp', 'wide'), may hold values from -6 to 6
- resid_grad: bfloat16 [4096, 8192], P('wide', 'tp'), may hold values from -6 to 6
- kv_grad: bfloat16 [4096, 2048], P('wide', 'tp'), may hold values from -6 to 6
- kv_weight: bfloat16 [8192, 2048], P('wide', 'tp'), may hold values from -0.125 to 0.125
- editor_in: bfloat16 [8192, 1920], P('tp'), may hold values from -0.0625 to 0.0625
- editor_bias: float32 [1920], replicated, may hold values from -3 to 3
- editor_gain: float32 [8192], P('tp'), may hold values from 0.5 to 1.5
- editor_out: bfloat16 [1920, 8192], P(None, 'tp'), may hold values from -0.125 to 0.125
- prompt_len: int32 [64], replicated, may hold values from 1 to 63
Outputs:
- weight_update: bfloat16 [28672, 8192], P('wide', 'tp')
All inputs are finite; a program needn't handle non-finite values.
Results may differ from a plain program's by a relative error of at most 0.0055.
Values may be sent and summed in bfloat16 or wider, within the bound.
No kernel may reach another device: no remote copies, remote signals or barrier semaphores. Data moves between devices by JAX's collectives and lax.ppermute only.
A program may use at most 128 MiB of HBM per device.

v0:
```python
import jax
import jax.numpy as jnp
from jax import lax
from jax.sharding import PartitionSpec as P

LEN = 64
EPSILON = 1e-06


def per_device(
    token_keys,
    resid_grad,
    kv_grad,
    kv_weight,
    editor_in,
    editor_bias,
    editor_gain,
    editor_out,
    prompt_len,
):
    own_rows = resid_grad.shape[0]
    local_width = resid_grad.shape[1]
    col_start = lax.axis_index("tp") * local_width
    partial_sum = lax.dot_general(
        kv_grad,
        lax.all_gather(kv_weight, "wide", axis=0, tiled=True),
        (((1,), (1,)), ((), ())),
        preferred_element_type=jnp.float32,
    )
    resid_float = resid_grad.astype(jnp.float32)
    own_cols = lax.dynamic_slice_in_dim(partial_sum, col_start, local_width, 1) + resid_float
    partial_sum = lax.dynamic_update_slice_in_dim(partial_sum, own_cols, col_start, 1)
    complete = lax.psum(partial_sum, "tp")
    gradient = lax.dynamic_slice_in_dim(complete, col_start, local_width, 1)
    squares = jnp.sum(complete * complete, axis=1, keepdims=True)
    scaled = (gradient * editor_gain).astype(jnp.bfloat16)
    hidden_part = jnp.dot(scaled, editor_in, preferred_element_type=jnp.float32)
    projected = lax.psum(hidden_part, "tp")
    full_width = local_width * lax.axis_size("tp")
    inv_rms = lax.rsqrt(squares / full_width + EPSILON)
    hidden = jnp.maximum(projected * inv_rms + editor_bias, 0.0).astype(jnp.bfloat16)
    local_examples = own_rows // LEN
    owner_starts = lax.dynamic_slice_in_dim(
        prompt_len, lax.axis_index("wide") * local_examples, local_examples, 0
    )
    starts = jnp.repeat(owner_starts, LEN, total_repeat_length=own_rows)
    position = jnp.arange(own_rows, dtype=jnp.int32) % LEN
    keep_mask = (position >= starts).astype(jnp.float32)
    edited = (
        (gradient + jnp.dot(hidden, editor_out, preferred_element_type=jnp.float32))
        * keep_mask[:, None]
    ).astype(jnp.bfloat16)
    edit_count = jnp.sum(LEN - prompt_len).astype(jnp.float32)
    key_table = lax.all_gather(token_keys, "tp", axis=0, tiled=True)
    initial = jnp.zeros((key_table.shape[1], local_width), jnp.float32)
    piece = lax.all_gather(edited, "wide", axis=0, tiled=True)
    key_block = lax.slice_in_dim(key_table, 0, piece.shape[0], axis=0)
    summed = initial + lax.dot_general(
        key_block, piece, (((0,), (0,)), ((), ())), preferred_element_type=jnp.float32
    )
    return (summed * lax.rsqrt(edit_count)).astype(jnp.bfloat16)


def solution(mesh):
    in_specs = (
        P("tp", "wide"),
        P("wide", "tp"),
        P("wide", "tp"),
        P("wide", "tp"),
        P("tp", None),
        P(),
        P("tp"),
        P(None, "tp"),
        P(),
    )
    out_specs = P("wide", "tp")
    return jax.shard_map(
        per_device, mesh=mesh, in_specs=in_specs, out_specs=out_specs, check_vma=False
    )
```

profile of v0, /device:TPU:35, one launch (start us, length us, event | category | flops | bytes accessed | tf_op | source)
XLA Modules:
  0.0 611.1 jit_solution(15675389544332909423)
XLA Ops:
  6.5 0.0 copy-start
  6.5 0.7 all-gather.4.cloned.1.call-update
  7.3 0.0 all-reduce.3.cloned.1.call-start
  7.3 0.0 copy-start.1
  7.3 65.0 %all-gather.4.cloned.1.call-done = bf16[8192,256]{1,0:T(8,128)(2,1)} async-done(((bf16[256,256]{1,0:T(8,128)(2,1)}), bf16[8192,256]{1,0:T(8,128)(2,1)}) %all-gather.4.cloned.1.call-update) | async-done | bytes 4194320 | tf_op jit(solution)/shard_map/all_gather | solution.py:26
  72.4 5.6 fusion.11
  78.0 1.9 add_dynamic-update-slice_fusion
  80.0 0.0 all-reduce.3.cloned.1.call-update
  80.0 0.0 copy-start.5
  80.0 0.0 copy-start.4
  80.0 0.0 all-reduce.5.cloned.1.call-start
  80.1 185.2 %all-reduce.3.cloned.1.call-done = f32[128,8192]{1,0:T(8,128)} async-done(((f32[128,8192]{1,0:T(8,128)}), f32[128,8192]{1,0:T(8,128)}) %all-reduce.3.cloned.1.call-update) | async-done | bytes 4194320 | tf_op jit(solution)/shard_map/psum | solution.py:33
  265.3 0.0 copy-done.3
  265.3 4.0 fusion.6
  269.2 0.0 all-reduce.5.cloned.1.call-update
  269.3 0.0 all-gather.8.cloned.1.call-start
  269.3 0.5 all-gather.8.cloned.1.call-update
  269.8 0.0 all-gather.6.cloned.1.call-start
  269.9 0.1 dynamic_slice.11
  270.0 0.7 fusion.10
  270.6 0.0 copy-done.4
  270.6 1.3 compare_convert_fusion
  271.9 2.5 multiply_reduce_fusion
  274.5 73.6 %all-reduce.5.cloned.1.call-done = f32[128,1920]{1,0:T(8,128)} async-done(((f32[128,1920]{1,0:T(8,128)}), f32[128,1920]{1,0:T(8,128)}) %all-reduce.5.cloned.1.call-update) | async-done | bytes 983056 | tf_op jit(solution)/shard_map/psum | solution.py:38
  348.0 0.0 copy-done.2
  348.0 4.0 fusion.2
  352.0 0.0 all-gather.6.cloned.1.call-update
  352.1 0.6 subtract_reduce_fusion
  353.3 153.2 %all-gather.8.cloned.1.call-done = bf16[4096,896]{1,0:T(8,128)(2,1)} async-done(((bf16[512,896]{1,0:T(8,128)(2,1)}), bf16[4096,896]{1,0:T(8,128)(2,1)}) %all-gather.8.cloned.1.call-update) | async-done | bytes 7340048 | tf_op jit(solution)/shard_map/all_gather | solution.py:54
  506.5 82.3 %all-gather.6.cloned.1.call-done = bf16[4096,1024]{1,0:T(8,128)(2,1)} async-done(((bf16[128,1024]{1,0:T(8,128)(2,1)}), bf16[4096,1024]{1,0:T(8,128)(2,1)}) %all-gather.6.cloned.1.call-update) | async-done | bytes 8388624 | tf_op jit(solution)/shard_map/all_gather | solution.py:56
  588.8 13.4 %fusion = bf16[896,1024]{0,1:T(8,128)(2,1)S(1)} fusion(f32[]{:T(128)S(6)} %rsqrt.12, bf16[4096,1024]{1,0:T(8,128)(2,1)} %all-gather.6.cloned.1.call-done, bf16[4096,896]{1,0:T(8,128)(2,1)} %all-gather.8.cloned.1.call-done), kind=kOutput, calls=%fused_computation.2 | convolution fusion | flops 7518027776 | bytes 17563652 | tf_op jit(solution)/shard_map/dot_general | solution.py:58
  602.2 2.4 copy.10
  (7 shorter events, 0.0 us)
Async XLA Ops:
  6.5 65.8 %copy-start = (bf16[128,256]{1,0:T(8,128)(2,1)S(1)}, bf16[128,256]{1,0:T(8,128)(2,1)}, u32[]{:S(2)}) copy-start(bf16[128,256]{1,0:T(8,128)(2,1)} %param.13) | copy-start | bytes 196612
  6.5 65.8 %all-gather.4.cloned.1.call-start = ((), (), s32[]{:S(2)}) async-start(), calls=%async_computation | async-start | bytes 4325376 | tf_op jit(solution)/shard_map/all_gather | solution.py:26
  7.3 258.0 %all-reduce.3.cloned.1.call-start = ((), (), s32[]{:S(2)}) async-start(), calls=%async_computation.1 | async-start | bytes 8388608 | tf_op jit(solution)/shard_map/psum | solution.py:33
  7.3 70.7 %copy-start.1 = (bf16[128,1024]{1,0:T(8,128)(2,1)S(1)}, bf16[128,1024]{1,0:T(8,128)(2,1)}, u32[]{:S(2)}) copy-start(bf16[128,1024]{1,0:T(8,128)(2,1)} %param.12) | copy-start | bytes 786436
  78.0 187.2 %copy-start.3 = (f32[1024]{0:T(1024)S(1)}, f32[1024]{0:T(1024)}, u32[]{:S(2)}) copy-start(f32[1024]{0:T(1024)} %param.17) | copy-start | bytes 12292
  80.0 189.9 %copy-start.5 = (s32[64]{0:T(128)S(1)}, s32[64]{0:T(128)}, u32[]{:S(2)}) copy-start(s32[64]{0:T(128)} %param.19) | copy-start | bytes 772
  80.0 190.6 %copy-start.4 = (pred[128]{0:T(512)(128)(4,1)S(1)}, pred[128]{0:T(512)(128)(4,1)}, u32[]{:S(2)}) copy-start(pred[128]{0:T(512)(128)(4,1)} %constant.120) | copy-start | bytes 388
  80.0 268.0 %all-reduce.5.cloned.1.call-start = ((), (), s32[]{:S(2)}) async-start(), calls=%async_computation.2 | async-start | bytes 1966080 | tf_op jit(solution)/shard_map/psum | solution.py:38
  269.2 78.8 %copy-start.2 = (f32[1920]{0:T(1024)S(1)}, f32[1920]{0:T(1024)}, u32[]{:S(2)}) copy-start(f32[1920]{0:T(1024)} %param.16) | copy-start | bytes 23044
  269.3 237.3 %all-gather.8.cloned.1.call-start = ((), (), s32[]{:S(2)}) async-start(), calls=%async_computation.4 | async-start | bytes 8257536 | tf_op jit(solution)/shard_map/all_gather | solution.py:54
  269.8 318.9 %all-gather.6.cloned.1.call-start = ((), (), s32[]{:S(2)}) async-start(), calls=%async_computation.3 | async-start | bytes 8650752 | tf_op jit(solution)/shard_map/all_gather | solution.py:56
Sparse Core Ops, SparseCore 0:
  9.9 62.4 all-gather.3
  80.1 185.1 all-reduce.2
  269.4 78.6 all-reduce.4
  349.7 156.7 all-gather.7
  508.9 79.8 all-gather.5
where the time goes:
time: 611 us
  waiting for transfers between devices  561 us (92%)
  matrix products  27 us (4%)
  between operations  13.8 us (2%)
  other arithmetic  6.35 us (1%)
    psum x1, waiting for transfers between devices, per_device(): complete = lax.psum(partial_sum, 'tp')  185 us
    all_gather x1, waiting for transfers between devices, per_device(): key_table = lax.all_gather(token_keys, 'tp', axis=0, tiled=True)  153 us
    all_gather x1, waiting for transfers between devices, per_device(): piece = lax.all_gather(edited, 'wide', axis=0, tiled=True)  82.3 us
    psum x1, waiting for transfers between devices, per_device(): projected = lax.psum(hidden_part, 'tp')  73.6 us
    all_gather x1, waiting for transfers between devices, per_device(): lax.all_gather(kv_weight, 'wide', axis=0, tiled=True)  65 us
    dot_general x1, matrix products, per_device(): lax.dot_general(key_block, piece, (((0,), (0,)), ((), ())), preferred_ele...  13.4 us
  transfers between devices with their start and end apart: 5, of which 5 were waited for; matrix products, arithmetic and copies ran while one was open for 1% of the time, Pallas kernels for 0%

commit v1 on v0

--- a/solution.py
+++ b/solution.py
@@ -53,7 +53,10 @@
     edit_count = jnp.sum(LEN - prompt_len).astype(jnp.float32)
     key_table = lax.all_gather(token_keys, "tp", axis=0, tiled=True)
     initial = jnp.zeros((key_table.shape[1], local_width), jnp.float32)
-    piece = lax.all_gather(edited, "wide", axis=0, tiled=True)
+    devices = lax.axis_size("wide")
+    blocks = jnp.stack([edited for _ in range(devices)])
+    blocks = lax.all_to_all(blocks, "wide", split_axis=0, concat_axis=0)
+    piece = jnp.concatenate(blocks, axis=0)
     key_block = lax.slice_in_dim(key_table, 0, piece.shape[0], axis=0)
     summed = initial + lax.dot_general(
         key_block, piece, (((0,), (0,)), ((), ())), preferred_element_type=jnp.float32

time: 611 us -> 715 us (1.17)
  waiting for transfers between devices: 561 us -> 645 us
  starting transfers between devices: 0.16 us -> 13.3 us
    all_gather x1, waiting for transfers between devices: 153 us -> 320 us  [per_device(): key_table = lax.all_gather(token_keys, 'tp', axis=0, tiled=True)]
    all_gather x1 -> x0, waiting for transfers between devices: 82.3 us -> none  [per_device(): piece = lax.all_gather(edited, 'wide', axis=0, tiled=True)]
    all_to_all x0 -> x1, starting transfers between devices: none -> 13.1 us  [per_device(): blocks = lax.all_to_all(blocks, 'wide', split_axis=0, concat_axis=0)]
  transfers between devices with their start and end apart: 5 -> 5, of which waited for: 5 -> 4; matrix products, arithmetic and copies ran while one was open for 1% -> 1% of each run, Pallas kernels for 0% -> 0%
where the time goes in v1:
time: 715 us; the launch traced here: 713 us
  waiting for transfers between devices  645 us (90%)
  matrix products  26.3 us (4%)
  between operations  13.9 us (2%)
  starting transfers between devices  13.3 us (2%)
  local copies, waits for them, and re-layouts  7.42 us (1%)
    all_gather x1, waiting for transfers between devices, per_device(): key_table = lax.all_gather(token_keys, 'tp', axis=0, tiled=True)  320 us
    psum x1, waiting for transfers between devices, per_device(): complete = lax.psum(partial_sum, 'tp')  185 us
    psum x1, waiting for transfers between devices, per_device(): projected = lax.psum(hidden_part, 'tp')  74.3 us
    all_gather x1, waiting for transfers between devices, per_device(): lax.all_gather(kv_weight, 'wide', axis=0, tiled=True)  65 us
  transfers between devices with their start and end apart: 5, of which 4 were waited for; matrix products, arithmetic and copies ran while one was open for 1% of the time, Pallas kernels for 0%

profile of v1, /device:TPU:35, one launch (start us, length us, event | category | flops | bytes accessed | tf_op | source)
XLA Modules:
  0.0 712.6 jit_solution(2202960528107667863)
XLA Ops:
  6.5 0.0 copy-start
  6.5 0.7 all-gather.3.cloned.1.call-update
  7.3 0.0 all-reduce.3.cloned.1.call-start
  7.3 0.0 copy-start.1
  7.3 65.0 %all-gather.3.cloned.1.call-done = bf16[8192,256]{1,0:T(8,128)(2,1)} async-done(((bf16[256,256]{1,0:T(8,128)(2,1)}), bf16[8192,256]{1,0:T(8,128)(2,1)}) %all-gather.3.cloned.1.call-update) | async-done | bytes 4194320 | tf_op jit(solution)/shard_map/all_gather | solution.py:26
  72.4 5.7 fusion.11
  78.0 1.9 add_dynamic-update-slice_fusion
  79.9 0.0 all-reduce.3.cloned.1.call-update
  80.0 0.0 copy-start.5
  80.0 0.0 copy-start.4
  80.0 0.0 copy-start.2
  80.0 0.0 all-reduce.5.cloned.1.call-start
  80.1 185.2 %all-reduce.3.cloned.1.call-done = f32[128,8192]{1,0:T(8,128)} async-done(((f32[128,8192]{1,0:T(8,128)}), f32[128,8192]{1,0:T(8,128)}) %all-reduce.3.cloned.1.call-update) | async-done | bytes 4194320 | tf_op jit(solution)/shard_map/psum | solution.py:33
  265.2 4.0 fusion.6
  269.2 0.0 all-reduce.5.cloned.1.call-update
  269.2 0.0 copy-done.5
  269.2 0.1 dynamic_slice.11
  269.3 0.6 fusion.10
  269.9 0.0 copy-done.4
  269.9 1.3 compare_convert_fusion
  271.2 2.5 multiply_reduce_fusion
  273.7 74.3 %all-reduce.5.cloned.1.call-done = f32[128,1920]{1,0:T(8,128)} async-done(((f32[128,1920]{1,0:T(8,128)}), f32[128,1920]{1,0:T(8,128)}) %all-reduce.5.cloned.1.call-update) | async-done | bytes 983056 | tf_op jit(solution)/shard_map/psum | solution.py:38
  348.0 3.3 fusion.2
  351.3 4.3 stack.2
  355.6 13.1 %all-to-all-start = ((bf16[32,128,1024]{2,1,0:T(8,128)(2,1)}), bf16[32,128,1024]{2,1,0:T(8,128)(2,1)}, u32[]{:S(2)}, u32[]{:S(2)}) async-start(bf16[32,128,1024]{2,1,0:T(8,128)(2,1)} %stack.2), calls=%async_computation | async-start | bytes 16777216 | tf_op jit(solution)/shard_map/all_to_all | solution.py:58
  368.8 0.0 all-gather.5.cloned.1.call-start
  368.8 0.5 all-gather.5.cloned.1.call-update
  369.3 0.6 subtract_reduce_fusion
  370.7 319.6 %all-gather.5.cloned.1.call-done = bf16[4096,896]{1,0:T(8,128)(2,1)} async-done(((bf16[512,896]{1,0:T(8,128)(2,1)}), bf16[4096,896]{1,0:T(8,128)(2,1)}) %all-gather.5.cloned.1.call-update) | async-done | bytes 7340048 | tf_op jit(solution)/shard_map/all_gather | solution.py:54
  690.3 0.0 all-to-all-done
  690.3 13.4 %fusion = bf16[896,1024]{0,1:T(8,128)(2,1)S(1)} fusion(f32[]{:T(128)S(6)} %rsqrt.12, bf16[4096,1024]{1,0:T(8,128)(2,1)} %bitcast.2, bf16[4096,896]{1,0:T(8,128)(2,1)} %all-gather.5.cloned.1.call-done), kind=kOutput, calls=%fused_computation.2 | convolution fusion | flops 7518027776 | bytes 17563652 | tf_op jit(solution)/shard_map/dot_general | solution.py:61
  703.7 2.4 copy.10
  (7 shorter events, 0.0 us)
Async XLA Ops:
  6.5 65.8 %copy-start = (bf16[128,256]{1,0:T(8,128)(2,1)S(1)}, bf16[128,256]{1,0:T(8,128)(2,1)}, u32[]{:S(2)}) copy-start(bf16[128,256]{1,0:T(8,128)(2,1)} %param.13) | copy-start | bytes 196612
  6.5 65.8 %all-gather.3.cloned.1.call-start = ((), (), s32[]{:S(2)}) async-start(), calls=%async_computation.1 | async-start | bytes 4325376 | tf_op jit(solution)/shard_map/all_gather | solution.py:26
  7.3 258.0 %all-reduce.3.cloned.1.call-start = ((), (), s32[]{:S(2)}) async-start(), calls=%async_computation.2 | async-start | bytes 8388608 | tf_op jit(solution)/shard_map/psum | solution.py:33
  7.3 70.7 %copy-start.1 = (bf16[128,1024]{1,0:T(8,128)(2,1)S(1)}, bf16[128,1024]{1,0:T(8,128)(2,1)}, u32[]{:S(2)}) copy-start(bf16[128,1024]{1,0:T(8,128)(2,1)} %param.12) | copy-start | bytes 786436
  78.0 187.2 %copy-start.3 = (f32[1024]{0:T(1024)S(1)}, f32[1024]{0:T(1024)}, u32[]{:S(2)}) copy-start(f32[1024]{0:T(1024)} %param.17) | copy-start | bytes 12292
  80.0 189.3 %copy-start.5 = (s32[64]{0:T(128)S(1)}, s32[64]{0:T(128)}, u32[]{:S(2)}) copy-start(s32[64]{0:T(128)} %param.19) | copy-start | bytes 772
  80.0 189.9 %copy-start.4 = (pred[128]{0:T(512)(128)(4,1)S(1)}, pred[128]{0:T(512)(128)(4,1)}, u32[]{:S(2)}) copy-start(pred[128]{0:T(512)(128)(4,1)} %constant.120) | copy-start | bytes 388
  80.0 268.0 %copy-start.2 = (f32[1920]{0:T(1024)S(1)}, f32[1920]{0:T(1024)}, u32[]{:S(2)}) copy-start(f32[1920]{0:T(1024)} %param.16) | copy-start | bytes 23044
  80.0 268.0 %all-reduce.5.cloned.1.call-start = ((), (), s32[]{:S(2)}) async-start(), calls=%async_computation.3 | async-start | bytes 1966080 | tf_op jit(solution)/shard_map/psum | solution.py:38
  355.6 334.6 %all-to-all-start = ((bf16[32,128,1024]{2,1,0:T(8,128)(2,1)}), bf16[32,128,1024]{2,1,0:T(8,128)(2,1)}, u32[]{:S(2)}, u32[]{:S(2)}) async-start(bf16[32,128,1024]{2,1,0:T(8,128)(2,1)} %stack.2), calls=%async_computation | async-start | bytes 16777216 | tf_op jit(solution)/shard_map/all_to_all | solution.py:58
  368.8 321.5 %all-gather.5.cloned.1.call-start = ((), (), s32[]{:S(2)}) async-start(), calls=%async_computation.4 | async-start | bytes 8257536 | tf_op jit(solution)/shard_map/all_gather | solution.py:54
Sparse Core Ops, SparseCore 0:
  9.9 62.4 all-gather.2
  80.1 185.1 all-reduce.2
  269.3 78.6 all-reduce.4
  371.1 319.1 all-gather.4

commit v2 on v0

--- a/solution.py
+++ b/solution.py
@@ -5,6 +5,11 @@
 
 LEN = 64
 EPSILON = 1e-06
+
+
+def gather_and_add(block, axis):
+    parts = lax.all_gather(block, axis)
+    return jnp.sum(parts, axis=0)
 
 
 def per_device(
@@ -35,7 +40,7 @@
     squares = jnp.sum(complete * complete, axis=1, keepdims=True)
     scaled = (gradient * editor_gain).astype(jnp.bfloat16)
     hidden_part = jnp.dot(scaled, editor_in, preferred_element_type=jnp.float32)
-    projected = lax.psum(hidden_part, "tp")
+    projected = gather_and_add(hidden_part, "tp")
     full_width = local_width * lax.axis_size("tp")
     inv_rms = lax.rsqrt(squares / full_width + EPSILON)
     hidden = jnp.maximum(projected * inv_rms + editor_bias, 0.0).astype(jnp.bfloat16)

time: 611 us -> 690 us (1.13)
  waiting for transfers between devices: 561 us -> 636 us
    all_gather x0 -> x1, waiting for transfers between devices: none -> 157 us  [gather_and_add(): parts = lax.all_gather(block, axis)]
    psum x1 -> x0, waiting for transfers between devices: 73.6 us -> none  [per_device(): projected = lax.psum(hidden_part, 'tp')]
    all_gather x1, waiting for transfers between devices: 153 us -> 145 us  [per_device(): key_table = lax.all_gather(token_keys, 'tp', axis=0, tiled=True)]
  transfers between devices with their start and end apart: 5 -> 5, of which waited for: 5 -> 5; matrix products, arithmetic and copies ran while one was open for 1% -> 2% of each run, Pallas kernels for 0% -> 0%
where the time goes in v2:
time: 690 us
  waiting for transfers between devices  636 us (92%)
  matrix products  26.7 us (4%)
  between operations  13.8 us (2%)
  other arithmetic  10.2 us (1%)
    psum x1, waiting for transfers between devices, per_device(): complete = lax.psum(partial_sum, 'tp')  185 us
    all_gather x1, waiting for transfers between devices, gather_and_add(): parts = lax.all_gather(block, axis)  157 us
    all_gather x1, waiting for transfers between devices, per_device(): key_table = lax.all_gather(token_keys, 'tp', axis=0, tiled=True)  145 us
    all_gather x1, waiting for transfers between devices, per_device(): piece = lax.all_gather(edited, 'wide', axis=0, tiled=True)  82.3 us
    all_gather x1, waiting for transfers between devices, per_device(): lax.all_gather(kv_weight, 'wide', axis=0, tiled=True)  65 us
  transfers between devices with their start and end apart: 5, of which 5 were waited for; matrix products, arithmetic and copies ran while one was open for 2% of the time, Pallas kernels for 0%

profile of v2, /device:TPU:35, one launch (start us, length us, event | category | flops | bytes accessed | tf_op | source)
XLA Modules:
  0.0 689.8 jit_solution(9113521425812279322)
XLA Ops:
  6.5 0.0 copy-start
  6.5 0.7 all-gather.6.cloned.1.call-update
  7.3 0.0 all-reduce.2.cloned.1.call-start
  7.3 0.0 copy-start.1
  7.3 65.0 %all-gather.6.cloned.1.call-done = bf16[8192,256]{1,0:T(8,128)(2,1)} async-done(((bf16[256,256]{1,0:T(8,128)(2,1)}), bf16[8192,256]{1,0:T(8,128)(2,1)}) %all-gather.6.cloned.1.call-update) | async-done | bytes 4194320 | tf_op jit(solution)/shard_map/all_gather | solution.py:31
  72.4 5.6 fusion.11
  78.0 1.9 add_dynamic-update-slice_fusion
  80.0 0.0 all-reduce.2.cloned.1.call-update
  80.0 0.0 copy-start.5
  80.0 0.0 copy-start.4
  80.0 0.0 all-gather.12.cloned.1.call-start
  80.0 185.2 %all-reduce.2.cloned.1.call-done = f32[128,8192]{1,0:T(8,128)} async-done(((f32[128,8192]{1,0:T(8,128)}), f32[128,8192]{1,0:T(8,128)}) %all-reduce.2.cloned.1.call-update) | async-done | bytes 4194320 | tf_op jit(solution)/shard_map/psum | solution.py:38
  265.2 4.0 fusion.6
  269.2 0.0 all-gather.12.cloned.1.call-update
  269.2 0.0 all-gather.10.cloned.1.call-start
  269.3 0.5 all-gather.10.cloned.1.call-update
  269.8 0.0 all-gather.8.cloned.1.call-start
  269.8 0.0 copy-done.5
  269.8 0.1 dynamic_slice.11
  269.9 0.7 fusion.10
  270.6 1.4 compare_convert_fusion
  272.0 2.5 multiply_reduce_fusion
  274.5 156.8 %all-gather.12.cloned.1.call-done = f32[1024,1920]{1,0:T(8,128)} async-done(((f32[128,1920]{1,0:T(8,128)}), f32[1024,1920]{1,0:T(8,128)}) %all-gather.12.cloned.1.call-update) | async-done | bytes 7864336 | tf_op jit(solution)/shard_map/all_gather | solution.py:11
  431.4 3.7 reduce_sum.27
  435.1 0.0 copy-done.2
  435.1 3.7 fusion.2
  438.8 0.0 all-gather.8.cloned.1.call-update
  438.8 0.6 subtract_reduce_fusion
  440.0 145.2 %all-gather.10.cloned.1.call-done = bf16[4096,896]{1,0:T(8,128)(2,1)} async-done(((bf16[512,896]{1,0:T(8,128)(2,1)}), bf16[4096,896]{1,0:T(8,128)(2,1)}) %all-gather.10.cloned.1.call-update) | async-done | bytes 7340048 | tf_op jit(solution)/shard_map/all_gather | solution.py:59
  585.2 82.3 %all-gather.8.cloned.1.call-done = bf16[4096,1024]{1,0:T(8,128)(2,1)} async-done(((bf16[128,1024]{1,0:T(8,128)(2,1)}), bf16[4096,1024]{1,0:T(8,128)(2,1)}) %all-gather.8.cloned.1.call-update) | async-done | bytes 8388624 | tf_op jit(solution)/shard_map/all_gather | solution.py:61
  667.5 13.4 %fusion = bf16[896,1024]{0,1:T(8,128)(2,1)S(1)} fusion(f32[]{:T(128)S(6)} %rsqrt.12, bf16[4096,1024]{1,0:T(8,128)(2,1)} %all-gather.8.cloned.1.call-done, bf16[4096,896]{1,0:T(8,128)(2,1)} %all-gather.10.cloned.1.call-done), kind=kOutput, calls=%fused_computation.2 | convolution fusion | flops 7518027776 | bytes 17563652 | tf_op jit(solution)/shard_map/dot_general | solution.py:63
  680.9 2.4 copy.10
  (8 shorter events, 0.0 us)
Async XLA Ops:
  6.5 65.8 %copy-start = (bf16[128,256]{1,0:T(8,128)(2,1)S(1)}, bf16[128,256]{1,0:T(8,128)(2,1)}, u32[]{:S(2)}) copy-start(bf16[128,256]{1,0:T(8,128)(2,1)} %param.13) | copy-start | bytes 196612
  6.5 65.8 %all-gather.6.cloned.1.call-start = ((), (), s32[]{:S(2)}) async-start(), calls=%async_computation | async-start | bytes 4325376 | tf_op jit(solution)/shard_map/all_gather | solution.py:31
  7.3 258.0 %all-reduce.2.cloned.1.call-start = ((), (), s32[]{:S(2)}) async-start(), calls=%async_computation.1 | async-start | bytes 8388608 | tf_op jit(solution)/shard_map/psum | solution.py:38
  7.3 70.7 %copy-start.1 = (bf16[128,1024]{1,0:T(8,128)(2,1)S(1)}, bf16[128,1024]{1,0:T(8,128)(2,1)}, u32[]{:S(2)}) copy-start(bf16[128,1024]{1,0:T(8,128)(2,1)} %param.12) | copy-start | bytes 786436
  78.0 187.2 %copy-start.3 = (f32[1024]{0:T(1024)S(1)}, f32[1024]{0:T(1024)}, u32[]{:S(2)}) copy-start(f32[1024]{0:T(1024)} %param.17) | copy-start | bytes 12292
  80.0 189.9 %copy-start.5 = (s32[64]{0:T(128)S(1)}, s32[64]{0:T(128)}, u32[]{:S(2)}) copy-start(s32[64]{0:T(128)} %param.19) | copy-start | bytes 772
  80.0 190.6 %copy-start.4 = (pred[128]{0:T(512)(128)(4,1)S(1)}, pred[128]{0:T(512)(128)(4,1)}, u32[]{:S(2)}) copy-start(pred[128]{0:T(512)(128)(4,1)} %constant.120) | copy-start | bytes 388
  80.0 351.4 %all-gather.12.cloned.1.call-start = ((), (), s32[]{:S(2)}) async-start(), calls=%async_computation.4 | async-start | bytes 8847360 | tf_op jit(solution)/shard_map/all_gather | solution.py:11
  269.2 316.0 %all-gather.10.cloned.1.call-start = ((), (), s32[]{:S(2)}) async-start(), calls=%async_computation.3 | async-start | bytes 8257536 | tf_op jit(solution)/shard_map/all_gather | solution.py:59
  269.8 397.7 %all-gather.8.cloned.1.call-start = ((), (), s32[]{:S(2)}) async-start(), calls=%async_computation.2 | async-start | bytes 8650752 | tf_op jit(solution)/shard_map/all_gather | solution.py:61
  431.4 3.7 copy-start.2
Sparse Core Ops, SparseCore 0:
  9.9 62.4 all-gather.5
  80.1 185.0 all-reduce.1
  269.3 161.9 all-gather.11
  433.0 152.1 all-gather.9
  587.6 79.8 all-gather.7
